TPU v7x, 32 devices: a whole 2x2x4 slice. The times are simulated.
32 devices in a mesh: fsdp: 2 (over y), ctx: 4 (over x, core), tp: 4 (over z).
Axes of the slice: x: 2, y: 2, z: 4, core: 2. Of those that a mesh axis runs over, the one named last changes fastest.
Arguments:
- tokens: bfloat16 [12608, 512], P(('fsdp', 'ctx', 'tp')), may hold values from -6 to 6
- w_qkv: float32 [512, 1536], P(('fsdp', 'ctx', 'tp')), may hold values from -0.375 to 0.375
- w_attend: float32 [512, 512], P(('fsdp', 'ctx', 'tp')), may hold values from -0.75 to 0.75
- w_route: float32 [512, 8], P(('fsdp', 'ctx', 'tp')), may hold values from -0.1875 to 0.1875
- gain_one: float32 [512], P(('fsdp', 'ctx', 'tp')), may hold values from 0.5 to 1.5
- shift_one: float32 [512], P(('fsdp', 'ctx', 'tp')), may hold values from -1 to 1
- gain_two: float32 [512], P(('fsdp', 'ctx', 'tp')), may hold values from 0.5 to 1.5
- shift_two: float32 [512], P(('fsdp', 'ctx', 'tp')), may hold values from -1 to 1
- w_up: float32 [8, 512, 2048], P(None, ('fsdp', 'ctx'), 'tp'), may hold values from -0.25 to 0.25
- w_down: float32 [8, 512, 2048], P(None, ('fsdp', 'ctx'), 'tp'), may hold values from -0.75 to 0.75
- routes: int32 [12608, 2], P(('fsdp', 'ctx')), may hold values from 0 to 7, all different within a row
- priority: int32 [8, 1576], P(('fsdp', 'ctx')), may hold values from 0 to 1575, each once within a row
- cotangent: bfloat16 [12608, 512], P(('fsdp', 'ctx', 'tp')), may hold values from -6 to 6
Outputs:
- output: bfloat16 [12608, 512], P(('fsdp', 'ctx', 'tp'))
- grad_tokens: bfloat16 [12608, 512], P(('fsdp', 'ctx', 'tp'))
- grad_qkv: float32 [512, 1536], P(('fsdp', 'ctx', 'tp'))
- grad_attend: float32 [512, 512], P(('fsdp', 'ctx', 'tp'))
- grad_route: float32 [512, 8], P(('fsdp', 'ctx', 'tp'))
- grad_gain_one: float32 [512], P(('fsdp', 'ctx', 'tp'))
- grad_shift_one: float32 [512], P(('fsdp', 'ctx', 'tp'))
- grad_gain_two: float32 [512], P(('fsdp', 'ctx', 'tp'))
- grad_shift_two: float32 [512], P(('fsdp', 'ctx', 'tp'))
- grad_up: float32 [8, 512, 2048], P(None, ('fsdp', 'ctx'), 'tp')
- grad_down: float32 [8, 512, 2048], P(None, ('fsdp', 'ctx'), 'tp')
Inputs may be any that keep to these rules, and one draw needn't show every extreme that they name: `routes`: each row names 2 different experts, and every expert is named by some row. `priority`: each row is a permutation of 0 to 1575.
All inputs are finite; a program needn't handle non-finite values.
Results may differ from a plain program's by a relative error of at most 0.015.
The roundings to bfloat16 on the way count: a program that leaves them out, or rounds other values in their place, can miss the bound.
Values may be sent and summed in bfloat16 or wider, within the bound.
No kernel may reach another device: no remote copies, remote signals or barrier semaphores. Data moves between devices by JAX's collectives and lax.ppermute only.
A program may use at most 192 MiB of HBM per device.

v0:
```python
from functools import partial
import math
import jax
import jax.numpy as jnp
from jax import lax
from jax.sharding import PartitionSpec as P

D = 512
HEADS = 8
HEAD = 64
SEQ = 197
TOP = 2
EXPERTS = 8
epsilon = 1e-06


def norm_forward(values):
    center = values - jnp.mean(values, axis=-1, keepdims=True)
    spread = jnp.mean(center * center, axis=-1, keepdims=True)
    inv_scale = lax.rsqrt(spread + epsilon)
    return (center * inv_scale, inv_scale)


def norm_backward(grad_norm, normed, inv_scale, gain_row):
    scaled = grad_norm * gain_row
    centred = scaled - jnp.mean(scaled, axis=-1, keepdims=True)
    return inv_scale * (centred - normed * jnp.mean(scaled * normed, axis=-1, keepdims=True))


def rows_product(left, right):
    return lax.dot_general(
        left, right, (((0,), (0,)), ((), ())), preferred_element_type=jnp.float32
    )


def times_transpose(left, right):
    return lax.dot_general(
        left, right, (((1,), (1,)), ((), ())), preferred_element_type=jnp.float32
    )


def slot_tables(routes_group, order_group, capacity):
    row_count = order_group.shape[0]
    inverse = (
        jnp.zeros((row_count,), jnp.int32)
        .at[order_group]
        .set(jnp.arange(row_count, dtype=jnp.int32))
    )
    ordered = routes_group[inverse].T.reshape(-1)
    expert_ids = jnp.arange(EXPERTS, dtype=jnp.int32)
    onehot = (ordered[:, None] == expert_ids[None, :]).astype(jnp.int32)
    earlier = jnp.cumsum(onehot, axis=0) - onehot
    slot_keyed = jnp.sum(earlier * onehot, axis=1).reshape(TOP, row_count)
    slot_index = slot_keyed[:, order_group].T
    kept_pair = slot_index < capacity
    position = jnp.where(kept_pair, routes_group * capacity + slot_index, 0)
    target = jnp.where(kept_pair, position, EXPERTS * capacity).reshape(-1)
    owners = jnp.broadcast_to(
        jnp.arange(row_count, dtype=jnp.int32)[:, None], (row_count, TOP)
    ).reshape(-1)
    slot_table = (
        jnp.full((EXPERTS * capacity,), row_count, jnp.int32).at[target].set(owners, mode="drop")
    )
    return (kept_pair, position, slot_table, target)


def fetch_experts(w_up, w_down):
    whole = (
        lax.all_gather(w_up.astype(jnp.bfloat16), ("fsdp", "ctx"), axis=1, tiled=True),
        lax.all_gather(w_down.astype(jnp.bfloat16), ("fsdp", "ctx"), axis=1, tiled=True),
    )
    return (whole[0], whole[1])


def on_device(
    tokens,
    w_qkv,
    w_attend,
    w_route,
    gain_one,
    shift_one,
    gain_two,
    shift_two,
    w_up,
    w_down,
    routes,
    priority,
    cotangent,
):
    tok_rows = tokens.shape[0]
    ctx_size = lax.axis_size("ctx")
    tp_size = lax.axis_size("tp")
    images = tok_rows // SEQ
    head_width = D // ctx_size
    local_heads = HEADS // ctx_size
    score_scale = 1.0 / math.sqrt(HEAD)
    group_rows = tok_rows * tp_size
    capacity = group_rows * TOP * 5 // (4 * EXPERTS)
    gathered = (
        lax.all_gather(w_qkv.astype(jnp.bfloat16), ("fsdp", "ctx", "tp"), axis=0, tiled=True),
        lax.all_gather(w_attend.astype(jnp.bfloat16), ("fsdp", "ctx", "tp"), axis=0, tiled=True),
        lax.all_gather(w_route.astype(jnp.bfloat16), ("fsdp", "ctx", "tp"), axis=0, tiled=True),
        lax.all_gather(gain_one.astype(jnp.bfloat16), ("fsdp", "ctx", "tp"), axis=0, tiled=True),
        lax.all_gather(shift_one.astype(jnp.bfloat16), ("fsdp", "ctx", "tp"), axis=0, tiled=True),
        lax.all_gather(gain_two.astype(jnp.bfloat16), ("fsdp", "ctx", "tp"), axis=0, tiled=True),
        lax.all_gather(shift_two.astype(jnp.bfloat16), ("fsdp", "ctx", "tp"), axis=0, tiled=True),
    )
    qkv_w = gathered[0]
    attend_w = gathered[1]
    route_w = gathered[2]
    gain_a = gathered[3].astype(jnp.float32)
    offset_a = gathered[4].astype(jnp.float32)
    gain_b = gathered[5].astype(jnp.float32)
    offset_b = gathered[6].astype(jnp.float32)
    inputs_f = tokens.astype(jnp.float32)
    normed_one, inv_one = norm_forward(inputs_f)
    a_one = (normed_one * gain_a + offset_a).astype(jnp.bfloat16)
    projected = jnp.dot(a_one, qkv_w, preferred_element_type=jnp.float32).astype(jnp.bfloat16)
    heads_local = projected.reshape(images, SEQ, 3, ctx_size, head_width)
    by_head = lax.all_to_all(heads_local, "ctx", split_axis=3, concat_axis=0, tiled=True)
    batch_images = by_head.shape[0]
    queries = by_head[:, :, 0, 0].reshape(batch_images, SEQ, local_heads, HEAD)
    keys_all = by_head[:, :, 1, 0].reshape(batch_images, SEQ, local_heads, HEAD)
    values_all = by_head[:, :, 2, 0].reshape(batch_images, SEQ, local_heads, HEAD)
    scores = (
        jnp.einsum("bqhd,bkhd->bhqk", queries, keys_all, preferred_element_type=jnp.float32)
        * score_scale
    )
    row_peak = jnp.max(scores, axis=-1, keepdims=True)
    log_total = row_peak + jnp.log(jnp.sum(jnp.exp(scores - row_peak), axis=-1, keepdims=True))
    weights_low = jnp.exp(scores - log_total).astype(jnp.bfloat16)
    context_heads = jnp.einsum(
        "bhqk,bkhd->bqhd", weights_low, values_all, preferred_element_type=jnp.float32
    ).astype(jnp.bfloat16)
    back_rows = lax.all_to_all(
        context_heads.reshape(batch_images, SEQ, 1, head_width),
        "ctx",
        split_axis=0,
        concat_axis=2,
        tiled=True,
    )
    context = back_rows.reshape(tok_rows, D)
    y_one = inputs_f + jnp.dot(context, attend_w, preferred_element_type=jnp.float32)
    normed_two, inv_two = norm_forward(y_one)
    a_two = (normed_two * gain_b + offset_b).astype(jnp.bfloat16)
    a_group, cot_group = (
        lax.all_gather(a_two, "tp", axis=0, tiled=True),
        lax.all_gather(cotangent, "tp", axis=0, tiled=True),
    )
    logits = jnp.dot(a_group, route_w, preferred_element_type=jnp.float32)
    gate_probs = jax.nn.softmax(logits, axis=-1)
    kept_pair, position, slot_table, flat_target = slot_tables(routes, priority[0], capacity)
    expert_ids = jnp.arange(EXPERTS, dtype=jnp.int32)
    route_onehot = (routes[:, :, None] == expert_ids[None, None, :]).astype(jnp.float32)
    weight_pair = jnp.where(kept_pair, jnp.sum(gate_probs[:, None, :] * route_onehot, axis=-1), 0.0)
    slot_gate = (
        jnp.zeros((EXPERTS * capacity,), jnp.float32)
        .at[flat_target]
        .set(weight_pair.reshape(-1), mode="drop")
    )
    local_count = EXPERTS
    pair_float = kept_pair.astype(jnp.float32)
    padded = jnp.concatenate([a_group, jnp.zeros((1, D), jnp.bfloat16)], axis=0)
    expert_in = padded[slot_table].reshape(local_count, capacity, D)
    up_w, down_w = fetch_experts(w_up, w_down)
    pre_act = jnp.einsum("ecd,edf->ecf", expert_in, up_w, preferred_element_type=jnp.float32)
    hidden = jax.nn.gelu(pre_act, approximate=True).astype(jnp.bfloat16)
    expert_out = jnp.einsum(
        "ecf,edf->ecd", hidden, down_w, preferred_element_type=jnp.float32
    ).reshape(local_count * capacity, D)
    picked = expert_out[position] * pair_float[:, :, None]
    combined = jnp.sum(picked * weight_pair[:, :, None], axis=1)
    moe_rows = lax.psum_scatter(
        combined.astype(jnp.bfloat16), "tp", scatter_dimension=0, tiled=True
    ).astype(jnp.float32)
    output = (y_one + moe_rows).astype(jnp.bfloat16)
    cot_float = cot_group.astype(jnp.float32)
    grad_weight = jnp.where(kept_pair, jnp.einsum("gjd,gd->gj", picked, cot_float), 0.0)
    cot_padded = jnp.concatenate([cot_group, jnp.zeros((1, D), jnp.bfloat16)], axis=0)
    grad_out = (
        (cot_padded[slot_table].astype(jnp.float32) * slot_gate[:, None])
        .astype(jnp.bfloat16)
        .reshape(local_count, capacity, D)
    )
    up_back, down_back = fetch_experts(w_up, w_down)
    grad_hidden = jnp.einsum(
        "ecd,edf->ecf", grad_out, down_back, preferred_element_type=jnp.float32
    )
    gelu_pull = jax.vjp(partial(jax.nn.gelu, approximate=True), pre_act)[1]
    grad_pre = gelu_pull(grad_hidden)[0].astype(jnp.bfloat16)
    grad_down_full = jnp.einsum(
        "ecd,ecf->edf", grad_out, hidden, preferred_element_type=jnp.float32
    )
    grad_up_full = jnp.einsum(
        "ecd,ecf->edf", expert_in, grad_pre, preferred_element_type=jnp.float32
    )
    grad_in = jnp.einsum(
        "ecf,edf->ecd", grad_pre, up_back, preferred_element_type=jnp.float32
    ).reshape(local_count * capacity, D)
    grad_group = jnp.sum(grad_in[position] * pair_float[:, :, None], axis=1)
    grad_moe, grad_weight_own = (
        lax.psum_scatter(grad_group, "tp", scatter_dimension=0, tiled=True),
        lax.psum_scatter(grad_weight, "tp", scatter_dimension=0, tiled=True),
    )
    start_row = lax.axis_index("tp") * tok_rows
    gates_own = lax.dynamic_slice_in_dim(gate_probs, start_row, tok_rows, 0)
    onehot_own = lax.dynamic_slice_in_dim(route_onehot, start_row, tok_rows, 0)
    grad_gates = jnp.sum(grad_weight_own[:, :, None] * onehot_own, axis=1)
    grad_logits = (
        gates_own * (grad_gates - jnp.sum(gates_own * grad_gates, axis=-1, keepdims=True))
    ).astype(jnp.bfloat16)
    grad_route_full = rows_product(a_two, grad_logits)
    grad_a_two = grad_moe + times_transpose(grad_logits, route_w)
    grad_gain_b = jnp.sum(grad_a_two * normed_two, axis=0)
    grad_offset_b = jnp.sum(grad_a_two, axis=0)
    grad_y_one = cotangent.astype(jnp.float32) + norm_backward(
        grad_a_two, normed_two, inv_two, gain_b
    )
    grad_branch = grad_y_one.astype(jnp.bfloat16)
    grad_attend_full = rows_product(context, grad_branch)
    grad_context = times_transpose(grad_branch, attend_w).astype(jnp.bfloat16)
    grad_heads = lax.all_to_all(
        grad_context.reshape(images, SEQ, ctx_size, head_width),
        "ctx",
        split_axis=2,
        concat_axis=0,
        tiled=True,
    )
    grad_heads = grad_heads.reshape(batch_images, SEQ, local_heads, HEAD)
    scores_again = (
        jnp.einsum("bqhd,bkhd->bhqk", queries, keys_all, preferred_element_type=jnp.float32)
        * score_scale
    )
    weights_again = jnp.exp(scores_again - log_total)
    grad_weights = jnp.einsum(
        "bqhd,bkhd->bhqk", grad_heads, values_all, preferred_element_type=jnp.float32
    )
    grad_values = jnp.einsum(
        "bhqk,bqhd->bkhd",
        weights_again.astype(jnp.bfloat16),
        grad_heads,
        preferred_element_type=jnp.float32,
    )
    row_dot = jnp.sum(weights_again * grad_weights, axis=-1, keepdims=True)
    grad_scores = (weights_again * (grad_weights - row_dot)).astype(jnp.bfloat16)
    grad_queries = (
        jnp.einsum("bhqk,bkhd->bqhd", grad_scores, keys_all, preferred_element_type=jnp.float32)
        * score_scale
    )
    grad_keys = (
        jnp.einsum("bhqk,bqhd->bkhd", grad_scores, queries, preferred_element_type=jnp.float32)
        * score_scale
    )
    grad_proj = jnp.stack([grad_queries, grad_keys, grad_values], axis=2).astype(jnp.bfloat16)
    grad_proj = grad_proj.reshape(batch_images, SEQ, 3, 1, head_width)
    grad_rows = lax.all_to_all(grad_proj, "ctx", split_axis=0, concat_axis=3, tiled=True).reshape(
        tok_rows, 3 * D
    )
    grad_qkv_full = rows_product(a_one, grad_rows)
    grad_a_one = times_transpose(grad_rows, qkv_w)
    grad_gain_a = jnp.sum(grad_a_one * normed_one, axis=0)
    grad_offset_a = jnp.sum(grad_a_one, axis=0)
    grad_tokens = (grad_y_one + norm_backward(grad_a_one, normed_one, inv_one, gain_a)).astype(
        jnp.bfloat16
    )
    summed = (
        lax.psum_scatter(grad_qkv_full, ("fsdp", "ctx", "tp"), scatter_dimension=0, tiled=True),
        lax.psum_scatter(grad_attend_full, ("fsdp", "ctx", "tp"), scatter_dimension=0, tiled=True),
        lax.psum_scatter(grad_route_full, ("fsdp", "ctx", "tp"), scatter_dimension=0, tiled=True),
        lax.psum_scatter(grad_gain_a, ("fsdp", "ctx", "tp"), scatter_dimension=0, tiled=True),
        lax.psum_scatter(grad_offset_a, ("fsdp", "ctx", "tp"), scatter_dimension=0, tiled=True),
        lax.psum_scatter(grad_gain_b, ("fsdp", "ctx", "tp"), scatter_dimension=0, tiled=True),
        lax.psum_scatter(grad_offset_b, ("fsdp", "ctx", "tp"), scatter_dimension=0, tiled=True),
    )
    grad_up_part, grad_down_part = (
        lax.psum_scatter(grad_up_full, ("fsdp", "ctx"), scatter_dimension=1, tiled=True),
        lax.psum_scatter(grad_down_full, ("fsdp", "ctx"), scatter_dimension=1, tiled=True),
    )
    return (
        output,
        grad_tokens,
        summed[0],
        summed[1],
        summed[2],
        summed[3],
        summed[4],
        summed[5],
        summed[6],
        grad_up_part,
        grad_down_part,
    )


def solution(mesh):
    in_specs = (
        P(("fsdp", "ctx", "tp"), None),
        P(("fsdp", "ctx", "tp"), None),
        P(("fsdp", "ctx", "tp"), None),
        P(("fsdp", "ctx", "tp"), None),
        P(("fsdp", "ctx", "tp")),
        P(("fsdp", "ctx", "tp")),
        P(("fsdp", "ctx", "tp")),
        P(("fsdp", "ctx", "tp")),
        P(None, ("fsdp", "ctx"), "tp"),
        P(None, ("fsdp", "ctx"), "tp"),
        P(("fsdp", "ctx"), None),
        P(("fsdp", "ctx"), None),
        P(("fsdp", "ctx", "tp"), None),
    )
    out_specs = (
        P(("fsdp", "ctx", "tp"), None),
        P(("fsdp", "ctx", "tp"), None),
        P(("fsdp", "ctx", "tp"), None),
        P(("fsdp", "ctx", "tp"), None),
        P(("fsdp", "ctx", "tp"), None),
        P(("fsdp", "ctx", "tp")),
        P(("fsdp", "ctx", "tp")),
        P(("fsdp", "ctx", "tp")),
        P(("fsdp", "ctx", "tp")),
        P(None, ("fsdp", "ctx"), "tp"),
        P(None, ("fsdp", "ctx"), "tp"),
    )
    return jax.shard_map(
        on_device, mesh=mesh, in_specs=in_specs, out_specs=out_specs, check_vma=False
    )
```

profile of v0, /device:TPU:0, one launch (start us, length us, event | category | flops | bytes accessed | tf_op | source)
XLA Modules:
  0.0 1153.1 jit_solution(11126072074795200958)
XLA Ops:
  13.1 42.1 %all-reduce.18 = (bf16[512]{0:T(512)(128)(2,1)S(1)}, bf16[512]{0:T(512)(128)(2,1)S(1)}, bf16[512]{0:T(512)(128)(2,1)S(1)}, bf16[512]{0:T(512)(128)(2,1)S(1)}) all-reduce(bf16[512]{0:T(512)(128)(2,1)S(1)} %dynamic-update-slice.1, bf16[512]{0:T(512)(128)(2,1)S(1)} %dynamic-update-slice, ...), channel_id=1, replica_groups=mesh['fsdp'=2,'ctx'=4,'tp'=4] {'fsdp','ctx','tp'}, use_global_device_ids=true, to_apply=%add.4 | all-reduce | flops 2048 | bytes 8192
  57.7 12.3 %all-gather.9.cloned.1.call-done = bf16[512,1536]{1,0:T(8,128)(2,1)} async-done(((bf16[16,1536]{1,0:T(8,128)(2,1)}), bf16[512,1536]{1,0:T(8,128)(2,1)}) %all-gather.9.cloned.1.call-update) | async-done | bytes 1572880 | tf_op jit(solution)/shard_map/all_gather | solution.py:100
  79.0 15.6 %all-to-all-done = bf16[2,197,3,4,128]{4,0,2,1,3:T(2,128)(2,1)S(1)} async-done(((bf16[2,197,3,4,128]{4,0,2,1,3:T(2,128)(2,1)}), bf16[2,197,3,4,128]{4,0,2,1,3:T(2,128)(2,1)S(1)}, u32[]{:S(2)}, u32[]{:S(2)}) %all-to-all-start) | async-done | bytes 1210400 | tf_op jit(solution)/shard_map/all_to_all | solution.py:120
  111.3 71.7 %all_gather.38 = bf16[512,512]{1,0:T(8,128)(2,1)S(1)} all-gather(bf16[16,512]{1,0:T(8,128)(2,1)S(1)} %convert_element_type.137), channel_id=1, replica_groups=mesh['fsdp'=2,'ctx'=4,'tp'=4] {'fsdp','ctx','tp'}, dimensions={0}, use_global_device_ids=true | all-gather | bytes 540672 | tf_op jit(solution)/shard_map/all_gather | solution.py:101
  189.6 66.0 %all-gather.1 = bf16[32,16,8]{1,2,0:T(8,128)(2,1)S(1)} all-gather(bf16[1,16,8]{1,2,0:T(8,128)(2,1)S(1)} %convert_bitcast_fusion.1), channel_id=1, replica_groups=mesh['fsdp'=2,'ctx'=4,'tp'=4] {'fsdp','ctx','tp'}, dimensions={0}, use_global_device_ids=true | all-gather | bytes 8448 | tf_op jit(solution)/shard_map/all_gather | solution.py:102
  278.4 15.8 %scatter_custom_fusion.1 = s32[3936]{0:T(1024)S(1)} fusion(s32[3152]{0:T(1024)S(1)} %fusion.42, s32[3152]{0:T(1024)S(1)} %reshape.330, s32[]{:T(128)} %constant.26.clone.1), kind=kCustom, calls=%fused_computation.109 | custom fusion | bytes 15748 | tf_op jit(solution)/shard_map/scatter | solution.py:62
  298.2 12.3 %gather_fusion.4 = bf16[3936,512]{1,0:T(8,128)(2,1)} fusion(bf16[1577,512]{1,0:T(8,128)(2,1)S(1)} %concatenate.15, s32[4096]{0:T(1024)S(1)} %pad_clamp_fusion.1), kind=kCustom, calls=%fused_computation.4 | custom fusion | bytes 8076672 | tf_op jit(solution)/shard_map/gather | solution.py:181
  323.1 12.4 %gather_fusion.2 = bf16[3936,512]{1,0:T(8,128)(2,1)} fusion(bf16[1577,512]{1,0:T(8,128)(2,1)S(1)} %concatenate.14, s32[4096]{0:T(1024)S(1)} %pad_clamp_fusion.1), kind=kCustom, calls=%fused_computation.2 | custom fusion | bytes 8076672 | tf_op jit(solution)/shard_map/gather | solution.py:164
  366.9 14.1 %gather_fusion.3 = f32[3152,512]{1,0:T(8,128)} fusion(f32[3936,512]{1,0:T(8,128)} %reshape.262, s32[4096]{0:T(1024)S(1)} %pad_clamp_fusion), kind=kCustom, calls=%fused_computation.3 | custom fusion | bytes 12923200 | tf_op jit(solution)/shard_map/gather | solution.py:171
  389.5 20.8 %fusion.10 = f32[1576,1,2]{2,1,0:T(1,128)S(1)} fusion(bf16[1576,512,1]{1,2,0:T(2,128)(2,1)S(1)} %copy-done.15, f32[1576,2,512]{2,1,0:T(2,128)} %reshape.295, f32[1576,2]{1,0:T(8,128)} %get-tuple-element.34), kind=kOutput, calls=%fused_computation.22 | convolution fusion | flops 4841472 | bytes 8094336 | tf_op jit(solution)/shard_map/gjd,gd->gj/dot_general | solution.py:178
  410.9 16.0 %scatter_custom_fusion.2 = f32[3936]{0:T(1024)S(1)} fusion(s32[3152]{0:T(1024)} %copy-done.34, f32[3152]{0:T(1024)S(1)} %reshape.338, f32[]{:T(128)} %constant.20.clone.1), kind=kCustom, calls=%fused_computation.107 | custom fusion | bytes 16256 | tf_op jit(solution)/shard_map/scatter | solution.py:159
  427.0 11.9 %fusion.9 = bf16[8,492,512]{2,1,0:T(8,128)(2,1)S(1)} fusion(f32[8,492,512]{2,1,0:T(8,128)} %fusion.61, bf16[8,512,512]{2,1,0:T(8,128)(2,1)} %all-gather.13.cloned.1.call-done, f32[8,492,512]{2,1,0:T(8,128)} %reshape.269, f32[8,492]{1,0:T(8,128)S(1)} %mul.246), kind=kOutput, calls=%fused_computation.17 | convolution fusion | flops 2107932672 | bytes 24362368 | tf_op jit(solution)/shard_map/ecd,edf->ecf/dot_general | solution.py:186
  453.5 14.1 %gather_fusion.5 = f32[3152,512]{1,0:T(8,128)} fusion(f32[3936,512]{1,0:T(8,128)} %reshape.264, s32[4096]{0:T(1024)S(1)} %pad_clamp_fusion), kind=kCustom, calls=%fused_computation.5 | custom fusion | bytes 12923200 | tf_op jit(solution)/shard_map/gather | solution.py:200
  476.0 20.3 %multiply_reduce_fusion = (f32[1576,512]{1,0:T(8,128)}, bf16[1576,512]{1,0:T(8,128)(2,1)S(1)}) fusion(f32[1576,2,512]{2,1,0:T(2,128)} %reshape.311, f32[1576,2]{1,0:T(8,128)} %get-tuple-element.34, f32[1576,2]{1,0:T(8,128)S(1)} %get-tuple-element.44, f32[1576,2,512]{2,1,0:T(2,128)} %reshape.295), kind=kLoop, calls=%fused_computation.20 | loop fusion | flops 6455296 | bytes 17777280 | tf_op jit(solution)/shard_map/reduce_sum | solution.py:200
  496.3 29.7 %fusion = bf16[400,512]{1,0:T(8,128)(2,1)S(1)} fusion(bf16[1576,512]{1,0:T(8,128)(2,1)S(1)} %get-tuple-element.20), kind=kCustom, calls=%all-reduce-scatter | all-reduce-scatter fusion | flops 819201 | bytes 2023936
  527.9 66.7 %fusion.56 = (f32[400,2]{1,0:T(8,128)S(1)}, f32[400,512]{1,0:T(8,128)S(1)}) fusion(f32[1576,2]{1,0:T(8,128)S(1)} %get-tuple-element.43, f32[1576,512]{1,0:T(8,128)} %get-tuple-element.19), kind=kCustom, calls=%all-reduce-scatter.3 | all-reduce-scatter fusion | flops 822401 | bytes 4063168
  645.2 19.0 %all_to_all.63 = bf16[8,197,3,1,128]{4,1,2,3,0:T(8,128)(2,1)S(1)} all-to-all(bf16[8,197,3,1,128]{4,1,2,3,0:T(8,128)(2,1)S(1)} %pad_maximum_fusion), channel_id=1, replica_groups=mesh['fsdp'=2,'ctx'=4,'tp'=4] {'ctx'}, dimensions={0} | all-to-all | bytes 2420736 | tf_op jit(solution)/shard_map/all_to_all | solution.py:256
  670.6 13.6 %fusion.14 = f32[8,512,512]{2,1,0:T(8,128)} fusion(f32[8,492,512]{2,1,0:T(8,128)} %reshape.269, f32[8,492]{1,0:T(8,128)S(1)} %copy-done.36, f32[8,492,512]{2,1,0:T(8,128)} %fusion.61), kind=kOutput, calls=%fused_computation.33 | convolution fusion | flops 2085765120 | bytes 24526208 | tf_op jit(solution)/shard_map/ecd,ecf->edf/dot_general | solution.py:191
  693.5 60.9 %reduce-scatter.22.cloned.1.call-done = f32[16,8]{1,0:T(8,128)} async-done(((f32[512,8]{1,0:T(8,128)}), f32[16,8]{1,0:T(8,128)}) %reduce-scatter.22.cloned.1.call-update) | async-done | bytes 528
  758.3 37.2 %all-reduce.17 = (f32[512]{0:T(512)S(1)}, f32[512]{0:T(512)S(1)}, f32[512]{0:T(512)S(1)}, f32[512]{0:T(512)S(1)}) all-reduce(f32[512]{0:T(512)S(1)} %get-tuple-element.13, f32[512]{0:T(512)S(1)} %get-tuple-element.18, f32[512]{0:T(512)S(1)} %get-tuple-element.11, ...), channel_id=8, replica_groups=mesh['fsdp'=2,'ctx'=4,'tp'=4] {'fsdp','ctx','tp'}, use_global_device_ids=true, to_apply=%region_31.32.clone | all-reduce | flops 2048 | bytes 16384
  798.8 91.7 %reduce-scatter.16.cloned.1.call-done = f32[16,512]{1,0:T(8,128)} async-done(((f32[512,512]{1,0:T(8,128)}), f32[16,512]{1,0:T(8,128)}) %reduce-scatter.16.cloned.1.call-update) | async-done | bytes 32784 | tf_op jit(solution)/shard_map/reduce_scatter | solution.py:268
  890.5 104.8 %reduce-scatter.14.cloned.1.call-done = f32[16,1536]{1,0:T(8,128)} async-done(((f32[512,1536]{1,0:T(8,128)}), f32[16,1536]{1,0:T(8,128)}) %reduce-scatter.14.cloned.1.call-update) | async-done | bytes 98320 | tf_op jit(solution)/shard_map/reduce_scatter | solution.py:267
  995.4 74.3 %reduce-scatter.20.cloned.1.call-done = f32[8,64,512]{2,1,0:T(8,128)} async-done(((f32[8,512,512]{2,1,0:T(8,128)}), f32[8,64,512]{2,1,0:T(8,128)}) %reduce-scatter.20.cloned.1.call-update) | async-done | bytes 1048592 | tf_op jit(solution)/shard_map/reduce_scatter | solution.py:277
  1069.7 75.3 %reduce-scatter.18.cloned.1.call-done = f32[8,64,512]{2,1,0:T(8,128)} async-done(((f32[8,512,512]{2,1,0:T(8,128)}), f32[8,64,512]{2,1,0:T(8,128)}) %reduce-scatter.18.cloned.1.call-update) | async-done | bytes 1048592 | tf_op jit(solution)/shard_map/reduce_scatter | solution.py:276
  (279 shorter events, 216.5 us)
Async XLA Ops:
  8.0 62.0 %all-gather.9.cloned.1.call-start = ((), (), s32[]{:S(2)}) async-start(), calls=%async_computation.9 | async-start | bytes 1622016 | tf_op jit(solution)/shard_map/all_gather | solution.py:100
  74.9 19.7 %all-to-all-start = ((bf16[2,197,3,4,128]{4,0,2,1,3:T(2,128)(2,1)}), bf16[2,197,3,4,128]{4,0,2,1,3:T(2,128)(2,1)S(1)}, u32[]{:S(2)}, u32[]{:S(2)}) async-start(bf16[2,197,3,4,128]{4,0,2,1,3:T(2,128)(2,1)} %copy.128), calls=%async_computation | async-start | bytes 2420736 | tf_op jit(solution)/shard_map/all_to_all | solution.py:120
  78.4 217.8 %all-gather.17.cloned.1.call-start = ((), (), s32[]{:S(2)}) async-start(), calls=%async_computation.17 | async-start | bytes 2048000 | tf_op jit(solution)/shard_map/all_gather | solution.py:148
  107.6 80.1 %copy-start.20 = (f32[8,64,512]{2,1,0:T(8,128)S(1)}, f32[8,64,512]{2,1,0:T(8,128)}, u32[]{:S(2)}) copy-start(f32[8,64,512]{2,1,0:T(8,128)} %param.21) | copy-start | bytes 3145732
  107.6 75.5 %all-to-all-start.1 = ((bf16[8,197,1,128]{3,1,2,0:T(8,128)(2,1)}), bf16[8,197,1,128]{3,1,2,0:T(8,128)(2,1)S(1)}, u32[]{:S(2)}, u32[]{:S(2)}) async-start(bf16[8,197,1,128]{3,1,2,0:T(8,128)(2,1)} %copy.134), calls=%async_computation.1 | async-start | bytes 819200 | tf_op jit(solution)/shard_map/all_to_all | solution.py:135
  111.2 208.0 %all-gather.15.cloned.1.call-start = ((), (), s32[]{:S(2)}) async-start(), calls=%async_computation.16 | async-start | bytes 2048000 | tf_op jit(solution)/shard_map/all_gather | solution.py:147
  111.3 77.3 %copy-start.28 = (f32[512]{0:T(512)}, f32[512]{0:T(512)S(1)}, u32[]{:S(2)}) copy-start(f32[512]{0:T(512)S(1)} %convert_element_type.139) | copy-start | bytes 6148
  111.3 77.3 %copy-start.37 = (f32[512]{0:T(512)}, f32[512]{0:T(512)S(1)}, u32[]{:S(2)}) copy-start(f32[512]{0:T(512)S(1)} %convert_element_type.141) | copy-start | bytes 6148
  187.6 152.7 %all-gather.11.cloned.1.call-start = ((), (), s32[]{:S(2)}) async-start(), calls=%async_computation.10 | async-start | bytes 4718592 | tf_op jit(solution)/shard_map/all_gather | solution.py:69
  188.6 160.7 %all-gather.13.cloned.1.call-start = ((), (), s32[]{:S(2)}) async-start(), calls=%async_computation.11 | async-start | bytes 4718592 | tf_op jit(solution)/shard_map/all_gather | solution.py:70
  526.1 75.4 %collective-permute-start = (bf16[18,512]{1,0:T(8,128)(2,1)S(1)}, bf16[18,512]{1,0:T(8,128)(2,1)S(1)}, u32[]{:S(2)}, u32[]{:S(2)}) collective-permute-start(bf16[18,512]{1,0:T(8,128)(2,1)S(1)} %slice.41), channel_id=1, source_target_pairs={{0,1},{1,2},{2,3},{4,5},{5,6},{6,7},{8,9},{9,10},{10,11},{12,13},{... | collective-permute-start | bytes 55304
  527.9 76.9 %copy-start.4 = (f32[394,512]{1,0:T(8,128)S(1)}, f32[394,512]{1,0:T(8,128)}, u32[]{:S(2)}) copy-start(f32[394,512]{1,0:T(8,128)} %copy-done.3) | copy-start | bytes 2420740
  527.9 76.9 %copy-start.26 = (f32[394]{0:T(512)S(1)}, f32[394]{0:T(512)}, u32[]{:S(2)}) copy-start(f32[394]{0:T(512)} %copy-done.25) | copy-start | bytes 4732
  527.9 76.9 %copy-start.29 = (f32[512]{0:T(512)S(1)}, f32[512]{0:T(512)}, u32[]{:S(2)}) copy-start(f32[512]{0:T(512)} %copy-done.28) | copy-start | bytes 6148
  527.9 76.9 %copy-start.31 = (f32[394]{0:T(512)S(1)}, f32[394]{0:T(512)}, u32[]{:S(2)}) copy-start(f32[394]{0:T(512)} %copy-done.30) | copy-start | bytes 4732
  594.7 4.9 collective-permute-start.2
  596.0 6.8 collective-permute-start.1
  613.8 11.7 %all-to-all-start.2 = ((bf16[2,197,4,128]{3,0,1,2:T(2,128)(2,1)}), bf16[2,197,4,128]{3,0,1,2:T(2,128)(2,1)}, u32[]{:S(2)}, u32[]{:S(2)}) async-start(bf16[2,197,4,128]{3,0,1,2:T(2,128)(2,1)} %copy.145), calls=%async_computation.2 | async-start | bytes 806912 | tf_op jit(solution)/shard_map/all_to_all | solution.py:222
  618.0 136.4 %reduce-scatter.22.cloned.1.call-start = ((), (), s32[]{:S(2)}) async-start(), calls=%async_computation.18 | async-start | bytes 270336
  620.4 270.2 %reduce-scatter.16.cloned.1.call-start = ((), (), s32[]{:S(2)}) async-start(), calls=%async_computation.13 | async-start | bytes 1081344 | tf_op jit(solution)/shard_map/reduce_scatter | solution.py:268
  623.2 372.2 %reduce-scatter.14.cloned.1.call-start = ((), (), s32[]{:S(2)}) async-start(), calls=%async_computation.12 | async-start | bytes 3244032 | tf_op jit(solution)/shard_map/reduce_scatter | solution.py:267
  670.3 399.4 %reduce-scatter.20.cloned.1.call-start = ((), (), s32[]{:S(2)}) async-start(), calls=%async_computation.15 | async-start | bytes 9437184 | tf_op jit(solution)/shard_map/reduce_scatter | solution.py:277
  684.2 460.8 %reduce-scatter.18.cloned.1.call-start = ((), (), s32[]{:S(2)}) async-start(), calls=%async_computation.14 | async-start | bytes 9437184 | tf_op jit(solution)/shard_map/reduce_scatter | solution.py:276
  693.5 104.2 %copy-start.8 = (f32[394,512]{1,0:T(8,128)S(1)}, f32[394,512]{1,0:T(8,128)}, u32[]{:S(2)}) copy-start(f32[394,512]{1,0:T(8,128)} %copy-done.7) | copy-start | bytes 2420740
  (40 other events, 789.5 us)
Sparse Core Ops, SparseCore 0:
  12.3 57.6 all-gather.8
  621.0 133.3 reduce-scatter.21
  757.2 133.2 reduce-scatter.15
  896.4 98.9 reduce-scatter.13
  999.3 70.4 reduce-scatter.19
  1073.6 71.3 reduce-scatter.17
Sparse Core Ops, SparseCore 1:
  80.5 39.0 all-gather.16
  187.7 35.3 all-gather.14
  224.9 35.3 all-gather.10
  262.2 36.4 all-gather.12
where the time goes:
time: 1160 us; the launch traced here: 1150 us
  waiting for transfers between devices  438 us (38%)
  blocking collectives  332 us (29%)
  local copies, waits for them, and re-layouts  192 us (17%)
  matrix products  112 us (10%)
  other arithmetic  41.9 us (4%)
  starting transfers between devices  18.6 us (2%)
  between operations  17.9 us (2%)
    unnamed x4, blocking collectives  176 us
    reduce_scatter x1, waiting for transfers between devices, on_device(): lax.psum_scatter(grad_qkv_full, ('fsdp', 'ctx', 'tp'), scatter_dimension=...  105 us
    reduce_scatter x1, waiting for transfers between devices, on_device(): lax.psum_scatter(grad_attend_full, ('fsdp', 'ctx', 'tp'), scatter_dimensi...  91.7 us
    reduce_scatter x1, waiting for transfers between devices, on_device(): lax.psum_scatter(grad_up_full, ('fsdp', 'ctx'), scatter_dimension=1, tile...  75.3 us
    reduce_scatter x1, waiting for transfers between devices, on_device(): lax.psum_scatter(grad_down_full, ('fsdp', 'ctx'), scatter_dimension=1, ti...  74.3 us
    all_gather x1, blocking collectives, on_device(): lax.all_gather(w_attend.astype(jnp.bfloat16), ('fsdp', 'ctx', 'tp'), axis...  71.7 us
    all_gather x1, blocking collectives, on_device(): lax.all_gather(w_route.astype(jnp.bfloat16), ('fsdp', 'ctx', 'tp'), axis=...  66 us
    unnamed x14, waiting for transfers between devices  61.5 us
  transfers between devices with their start and end apart: 16, of which 8 were waited for; matrix products, arithmetic and copies ran while one was open for 21% of the time, Pallas kernels for 0%

commit v1 on v0

--- a/solution.py
+++ b/solution.py
@@ -4,6 +4,7 @@
 import jax.numpy as jnp
 from jax import lax
 from jax.sharding import PartitionSpec as P
+from jax.lax import axis_index, axis_size, ppermute
 
 D = 512
 HEADS = 8
@@ -12,6 +13,29 @@
 TOP = 2
 EXPERTS = 8
 epsilon = 1e-06
+
+
+def lay_heaps(buf):
+    z_new, y_new, carry_out = (
+        axis_size(("fsdp", "ctx", "tp")),
+        axis_index(("fsdp", "ctx", "tp")),
+        buf.shape[0],
+    )
+    mixed_arr, piece_next = (buf, 1)
+    while piece_next < z_new:
+        mixed_arr = jnp.concatenate(
+            [
+                mixed_arr,
+                ppermute(
+                    mixed_arr,
+                    axis_name=("fsdp", "ctx", "tp"),
+                    perm=tuple(((at, (at - piece_next) % z_new) for at in range(z_new))),
+                ),
+            ],
+            axis=0,
+        )
+        piece_next = 2 * piece_next
+    return jnp.roll(mixed_arr, shift=y_new * carry_out, axis=0)
 
 
 def norm_forward(values):
@@ -98,7 +122,7 @@
     capacity = group_rows * TOP * 5 // (4 * EXPERTS)
     gathered = (
         lax.all_gather(w_qkv.astype(jnp.bfloat16), ("fsdp", "ctx", "tp"), axis=0, tiled=True),
-        lax.all_gather(w_attend.astype(jnp.bfloat16), ("fsdp", "ctx", "tp"), axis=0, tiled=True),
+        lay_heaps(w_attend.astype(jnp.bfloat16)),
         lax.all_gather(w_route.astype(jnp.bfloat16), ("fsdp", "ctx", "tp"), axis=0, tiled=True),
         lax.all_gather(gain_one.astype(jnp.bfloat16), ("fsdp", "ctx", "tp"), axis=0, tiled=True),
         lax.all_gather(shift_one.astype(jnp.bfloat16), ("fsdp", "ctx", "tp"), axis=0, tiled=True),

time: 1160 us -> 1110 us (0.957)
  blocking collectives: 332 us -> 258 us
  starting transfers between devices: 18.6 us -> 33.2 us
    all_gather x1 -> x0, blocking collectives: 71.7 us -> none  [on_device(): lax.all_gather(w_attend.astype(jnp.bfloat16), ('fsdp', 'ctx', 'tp'), axis...]
    ppermute x0 -> x5, starting transfers between devices: none -> 13.7 us  [lay_heaps(): ppermute(mixed_arr, axis_name=('fsdp', 'ctx', 'tp'), perm=tuple(((at, (at...]
    all_gather x1, waiting for transfers between devices: 12.3 us -> 0.01 us  [on_device(): lax.all_gather(w_qkv.astype(jnp.bfloat16), ('fsdp', 'ctx', 'tp'), axis=0,...]
    unnamed x125 -> x155, local copies, waits for them, and re-layouts: 22.4 us -> 27.6 us
  transfers between devices with their start and end apart: 16 -> 21, of which waited for: 8 -> 11; matrix products, arithmetic and copies ran while one was open for 21% -> 24% of each run, Pallas kernels for 0% -> 0%
where the time goes in v1:
time: 1110 us; the launch traced here: 1090 us
  waiting for transfers between devices  430 us (39%)
  blocking collectives  258 us (23%)
  local copies, waits for them, and re-layouts  199 us (18%)
  matrix products  112 us (10%)
  other arithmetic  44 us (4%)
  starting transfers between devices  33.2 us (3%)
  between operations  18.1 us (2%)
    unnamed x4, blocking collectives  170 us
    reduce_scatter x1, waiting for transfers between devices, on_device(): lax.psum_scatter(grad_qkv_full, ('fsdp', 'ctx', 'tp'), scatter_dimension=...  105 us
    reduce_scatter x1, waiting for transfers between devices, on_device(): lax.psum_scatter(grad_attend_full, ('fsdp', 'ctx', 'tp'), scatter_dimensi...  91.7 us
    reduce_scatter x1, waiting for transfers between devices, on_device(): lax.psum_scatter(grad_up_full, ('fsdp', 'ctx'), scatter_dimension=1, tile...  75.3 us
    reduce_scatter x1, waiting for transfers between devices, on_device(): lax.psum_scatter(grad_down_full, ('fsdp', 'ctx'), scatter_dimension=1, ti...  74.3 us
    all_gather x1, blocking collectives, on_device(): lax.all_gather(w_route.astype(jnp.bfloat16), ('fsdp', 'ctx', 'tp'), axis=...  69.7 us
    unnamed x14, waiting for transfers between devices  62.2 us
    unnamed x155, local copies, waits for them, and re-layouts  27.6 us
  transfers between devices with their start and end apart: 21, of which 11 were waited for; matrix products, arithmetic and copies ran while one was open for 24% of the time, Pallas kernels for 0%

profile of v1, /device:TPU:0, one launch (start us, length us, event | category | flops | bytes accessed | tf_op | source)
XLA Modules:
  0.0 1095.0 jit_solution(273838462007111988)
XLA Ops:
  23.3 37.0 %all-reduce.18 = (bf16[512]{0:T(512)(128)(2,1)S(1)}, bf16[512]{0:T(512)(128)(2,1)S(1)}, bf16[512]{0:T(512)(128)(2,1)}, bf16[512]{0:T(512)(128)(2,1)}) all-reduce(bf16[512]{0:T(512)(128)(2,1)S(1)} %dynamic-update-slice.1, bf16[512]{0:T(512)(128)(2,1)S(1)} %dynamic-update-slice, ...), channel_id=1, replica_groups=mesh['fsdp'=2,'ctx'=4,'tp'=4] {'fsdp','ctx','tp'}, use_global_device_ids=true, to_apply=%add.4 | all-reduce | flops 2048 | bytes 8192
  126.9 69.7 %all-gather.1 = bf16[32,16,8]{1,2,0:T(8,128)(2,1)S(1)} all-gather(bf16[1,16,8]{1,2,0:T(8,128)(2,1)S(1)} %convert_bitcast_fusion.1), channel_id=1, replica_groups=mesh['fsdp'=2,'ctx'=4,'tp'=4] {'fsdp','ctx','tp'}, dimensions={0}, use_global_device_ids=true | all-gather | bytes 8448 | tf_op jit(solution)/shard_map/all_gather | solution.py:126
  197.1 9.1 scatter_custom_fusion
  219.4 15.8 %scatter_custom_fusion.1 = s32[3936]{0:T(1024)S(1)} fusion(s32[3152]{0:T(1024)S(1)} %fusion.44, s32[3152]{0:T(1024)S(1)} %reshape.330, s32[]{:T(128)} %constant.88.clone.1), kind=kCustom, calls=%fused_computation.131 | custom fusion | bytes 15748 | tf_op jit(solution)/shard_map/scatter | solution.py:86
  239.2 12.4 %gather_fusion.4 = bf16[3936,512]{1,0:T(8,128)(2,1)} fusion(bf16[1577,512]{1,0:T(8,128)(2,1)S(1)} %concatenate.42, s32[4096]{0:T(1024)S(1)} %pad_clamp_fusion.1), kind=kCustom, calls=%fused_computation.4 | custom fusion | bytes 8076672 | tf_op jit(solution)/shard_map/gather | solution.py:205
  264.1 12.3 %gather_fusion.2 = bf16[3936,512]{1,0:T(8,128)(2,1)} fusion(bf16[1577,512]{1,0:T(8,128)(2,1)S(1)} %concatenate.41, s32[4096]{0:T(1024)S(1)} %pad_clamp_fusion.1), kind=kCustom, calls=%fused_computation.2 | custom fusion | bytes 8076672 | tf_op jit(solution)/shard_map/gather | solution.py:188
  290.2 10.4 fusion.59
  307.7 14.2 %gather_fusion.3 = f32[3152,512]{1,0:T(8,128)} fusion(f32[3936,512]{1,0:T(8,128)} %reshape.262, s32[4096]{0:T(1024)S(1)} %pad_clamp_fusion), kind=kCustom, calls=%fused_computation.3 | custom fusion | bytes 12923200 | tf_op jit(solution)/shard_map/gather | solution.py:195
  330.4 20.8 %fusion.10 = f32[1576,1,2]{2,1,0:T(1,128)S(1)} fusion(bf16[1576,512,1]{1,2,0:T(2,128)(2,1)S(1)} %copy-done.13, f32[1576,2,512]{2,1,0:T(2,128)} %reshape.295, f32[1576,2]{1,0:T(8,128)} %get-tuple-element.34), kind=kOutput, calls=%fused_computation.22 | convolution fusion | flops 4841472 | bytes 8094336 | tf_op jit(solution)/shard_map/gjd,gd->gj/dot_general | solution.py:202
  351.8 16.0 %scatter_custom_fusion.2 = f32[3936]{0:T(1024)S(1)} fusion(s32[3152]{0:T(1024)} %copy-done.43, f32[3152]{0:T(1024)S(1)} %reshape.338, f32[]{:T(128)} %constant.32.clone.1), kind=kCustom, calls=%fused_computation.129 | custom fusion | bytes 16256 | tf_op jit(solution)/shard_map/scatter | solution.py:183
  367.9 11.9 %fusion.9 = bf16[8,492,512]{2,1,0:T(8,128)(2,1)S(1)} fusion(f32[8,492,512]{2,1,0:T(8,128)} %fusion.65, bf16[8,512,512]{2,1,0:T(8,128)(2,1)} %all-gather.13.cloned.1.call-done, f32[8,492,512]{2,1,0:T(8,128)} %reshape.269, f32[8,492]{1,0:T(8,128)S(1)} %mul.258), kind=kOutput, calls=%fused_computation.17 | convolution fusion | flops 2107932672 | bytes 24362368 | tf_op jit(solution)/shard_map/ecd,edf->ecf/dot_general | solution.py:210
  394.4 14.1 %gather_fusion.5 = f32[3152,512]{1,0:T(8,128)} fusion(f32[3936,512]{1,0:T(8,128)} %reshape.264, s32[4096]{0:T(1024)S(1)} %pad_clamp_fusion), kind=kCustom, calls=%fused_computation.5 | custom fusion | bytes 12923200 | tf_op jit(solution)/shard_map/gather | solution.py:224
  416.8 20.3 %multiply_reduce_fusion = (f32[1576,512]{1,0:T(8,128)}, bf16[1576,512]{1,0:T(8,128)(2,1)S(1)}) fusion(f32[1576,2,512]{2,1,0:T(2,128)} %reshape.311, f32[1576,2]{1,0:T(8,128)} %get-tuple-element.34, f32[1576,2]{1,0:T(8,128)S(1)} %get-tuple-element.46, f32[1576,2,512]{2,1,0:T(2,128)} %reshape.295), kind=kLoop, calls=%fused_computation.20 | loop fusion | flops 6455296 | bytes 17777280 | tf_op jit(solution)/shard_map/reduce_sum | solution.py:224
  437.2 27.7 %fusion = bf16[400,512]{1,0:T(8,128)(2,1)S(1)} fusion(bf16[1576,512]{1,0:T(8,128)(2,1)S(1)} %get-tuple-element.20), kind=kCustom, calls=%all-reduce-scatter | all-reduce-scatter fusion | flops 819201 | bytes 2023936
  467.5 67.7 %fusion.60 = (f32[400,2]{1,0:T(8,128)S(1)}, f32[400,512]{1,0:T(8,128)S(1)}) fusion(f32[1576,2]{1,0:T(8,128)S(1)} %get-tuple-element.45, f32[1576,512]{1,0:T(8,128)} %get-tuple-element.19), kind=kCustom, calls=%all-reduce-scatter.3 | all-reduce-scatter fusion | flops 822401 | bytes 4063168
  585.7 19.0 %all_to_all.63 = bf16[8,197,3,1,128]{4,1,2,3,0:T(8,128)(2,1)S(1)} all-to-all(bf16[8,197,3,1,128]{4,1,2,3,0:T(8,128)(2,1)S(1)} %pad_maximum_fusion), channel_id=1, replica_groups=mesh['fsdp'=2,'ctx'=4,'tp'=4] {'ctx'}, dimensions={0} | all-to-all | bytes 2420736 | tf_op jit(solution)/shard_map/all_to_all | solution.py:280
  611.2 13.6 %fusion.14 = f32[8,512,512]{2,1,0:T(8,128)} fusion(f32[8,492,512]{2,1,0:T(8,128)} %reshape.269, f32[8,492]{1,0:T(8,128)S(1)} %mul.258, f32[8,492,512]{2,1,0:T(8,128)} %fusion.65), kind=kOutput, calls=%fused_computation.33 | convolution fusion | flops 2085765120 | bytes 24526208 | tf_op jit(solution)/shard_map/ecd,ecf->edf/dot_general | solution.py:215
  624.8 9.2 fusion.68
  634.1 62.0 %reduce-scatter.22.cloned.1.call-done = f32[16,8]{1,0:T(8,128)} async-done(((f32[512,8]{1,0:T(8,128)}), f32[16,8]{1,0:T(8,128)}) %reduce-scatter.22.cloned.1.call-update) | async-done | bytes 528
  700.0 37.1 %all-reduce.17 = (f32[512]{0:T(512)S(1)}, f32[512]{0:T(512)S(1)}, f32[512]{0:T(512)S(1)}, f32[512]{0:T(512)S(1)}) all-reduce(f32[512]{0:T(512)S(1)} %get-tuple-element.13, f32[512]{0:T(512)S(1)} %get-tuple-element.18, f32[512]{0:T(512)S(1)} %get-tuple-element.11, ...), channel_id=8, replica_groups=mesh['fsdp'=2,'ctx'=4,'tp'=4] {'fsdp','ctx','tp'}, use_global_device_ids=true, to_apply=%region_31.32.clone | all-reduce | flops 2048 | bytes 16384
  740.5 91.7 %reduce-scatter.16.cloned.1.call-done = f32[16,512]{1,0:T(8,128)} async-done(((f32[512,512]{1,0:T(8,128)}), f32[16,512]{1,0:T(8,128)}) %reduce-scatter.16.cloned.1.call-update) | async-done | bytes 32784 | tf_op jit(solution)/shard_map/reduce_scatter | solution.py:292
  832.3 105.1 %reduce-scatter.14.cloned.1.call-done = f32[16,1536]{1,0:T(8,128)} async-done(((f32[512,1536]{1,0:T(8,128)}), f32[16,1536]{1,0:T(8,128)}) %reduce-scatter.14.cloned.1.call-update) | async-done | bytes 98320 | tf_op jit(solution)/shard_map/reduce_scatter | solution.py:291
  937.3 74.3 %reduce-scatter.20.cloned.1.call-done = f32[8,64,512]{2,1,0:T(8,128)} async-done(((f32[8,512,512]{2,1,0:T(8,128)}), f32[8,64,512]{2,1,0:T(8,128)}) %reduce-scatter.20.cloned.1.call-update) | async-done | bytes 1048592 | tf_op jit(solution)/shard_map/reduce_scatter | solution.py:301
  1011.6 75.3 %reduce-scatter.18.cloned.1.call-done = f32[8,64,512]{2,1,0:T(8,128)} async-done(((f32[8,512,512]{2,1,0:T(8,128)}), f32[8,64,512]{2,1,0:T(8,128)}) %reduce-scatter.18.cloned.1.call-update) | async-done | bytes 1048592 | tf_op jit(solution)/shard_map/reduce_scatter | solution.py:300
  (323 shorter events, 230.1 us)
Async XLA Ops:
  8.0 63.4 %all-gather.9.cloned.1.call-start = ((), (), s32[]{:S(2)}) async-start(), calls=%async_computation.9 | async-start | bytes 1622016 | tf_op jit(solution)/shard_map/all_gather | solution.py:124
  11.0 49.4 %collective-permute-start = (bf16[16,512]{1,0:T(8,128)(2,1)S(1)}, bf16[16,512]{1,0:T(8,128)(2,1)S(1)}, u32[]{:S(2)}, u32[]{:S(2)}) collective-permute-start(bf16[16,512]{1,0:T(8,128)(2,1)S(1)} %get-tuple-element.37), channel_id=1, source_target_pairs={{0,31},{1,0},{2,1},{3,2},{4,3},{5,4},{6,5},{7,6},{8,7},{9,8},{10,9... | collective-permute-start | bytes 49160 | tf_op jit(solution)/shard_map/ppermute | solution.py:29
  60.4 5.6 collective-permute-start.1
  66.1 2.5 collective-permute-start.2
  69.2 10.8 collective-permute-start.3
  76.4 19.7 %all-to-all-start = ((bf16[2,197,3,4,128]{4,0,2,1,3:T(2,128)(2,1)}), bf16[2,197,3,4,128]{4,0,2,1,3:T(2,128)(2,1)S(1)}, u32[]{:S(2)}, u32[]{:S(2)}) async-start(bf16[2,197,3,4,128]{4,0,2,1,3:T(2,128)(2,1)} %copy.128), calls=%async_computation | async-start | bytes 2420736 | tf_op jit(solution)/shard_map/all_to_all | solution.py:144
  79.9 157.2 %all-gather.17.cloned.1.call-start = ((), (), s32[]{:S(2)}) async-start(), calls=%async_computation.17 | async-start | bytes 2048000 | tf_op jit(solution)/shard_map/all_gather | solution.py:172
  81.0 8.8 collective-permute-start.4
  109.2 11.0 %all-to-all-start.1 = ((bf16[8,197,1,128]{3,1,2,0:T(8,128)(2,1)}), bf16[8,197,1,128]{3,1,2,0:T(8,128)(2,1)S(1)}, u32[]{:S(2)}, u32[]{:S(2)}) async-start(bf16[8,197,1,128]{3,1,2,0:T(8,128)(2,1)} %copy.134), calls=%async_computation.1 | async-start | bytes 819200 | tf_op jit(solution)/shard_map/all_to_all | solution.py:159
  112.7 147.5 %all-gather.15.cloned.1.call-start = ((), (), s32[]{:S(2)}) async-start(), calls=%async_computation.16 | async-start | bytes 2048000 | tf_op jit(solution)/shard_map/all_gather | solution.py:171
  123.1 86.2 %copy-start.35 = (f32[394]{0:T(512)}, f32[394]{0:T(512)S(1)}, u32[]{:S(2)}) copy-start(f32[394]{0:T(512)S(1)} %broadcast_multiply_fusion.5) | copy-start | bytes 4732
  125.0 156.3 %all-gather.11.cloned.1.call-start = ((), (), s32[]{:S(2)}) async-start(), calls=%async_computation.10 | async-start | bytes 4718592 | tf_op jit(solution)/shard_map/all_gather | solution.py:93
  125.9 164.3 %all-gather.13.cloned.1.call-start = ((), (), s32[]{:S(2)}) async-start(), calls=%async_computation.11 | async-start | bytes 4718592 | tf_op jit(solution)/shard_map/all_gather | solution.py:94
  464.9 77.5 %collective-permute-start.5 = (bf16[18,512]{1,0:T(8,128)(2,1)S(1)}, bf16[18,512]{1,0:T(8,128)(2,1)}, u32[]{:S(2)}, u32[]{:S(2)}) collective-permute-start(bf16[18,512]{1,0:T(8,128)(2,1)S(1)} %slice.41), channel_id=1, source_target_pairs={{0,1},{1,2},{2,3},{4,5},{5,6},{6,7},{8,9},{9,10},{10,11},{12,13},{... | collective-permute-start | bytes 55304
  467.4 78.9 %copy-start.38 = (f32[512]{0:T(512)S(1)}, f32[512]{0:T(512)}, u32[]{:S(2)}) copy-start(f32[512]{0:T(512)} %convert_element_type.139) | copy-start | bytes 6148
  535.2 5.3 collective-permute-start.7
  537.6 6.7 collective-permute-start.6
  554.4 11.7 %all-to-all-start.2 = ((bf16[2,197,4,128]{3,0,1,2:T(2,128)(2,1)}), bf16[2,197,4,128]{3,0,1,2:T(2,128)(2,1)}, u32[]{:S(2)}, u32[]{:S(2)}) async-start(bf16[2,197,4,128]{3,0,1,2:T(2,128)(2,1)} %copy.145), calls=%async_computation.2 | async-start | bytes 806912 | tf_op jit(solution)/shard_map/all_to_all | solution.py:246
  558.5 137.6 %reduce-scatter.22.cloned.1.call-start = ((), (), s32[]{:S(2)}) async-start(), calls=%async_computation.18 | async-start | bytes 270336
  560.9 271.4 %reduce-scatter.16.cloned.1.call-start = ((), (), s32[]{:S(2)}) async-start(), calls=%async_computation.13 | async-start | bytes 1081344 | tf_op jit(solution)/shard_map/reduce_scatter | solution.py:292
  563.7 373.6 %reduce-scatter.14.cloned.1.call-start = ((), (), s32[]{:S(2)}) async-start(), calls=%async_computation.12 | async-start | bytes 3244032 | tf_op jit(solution)/shard_map/reduce_scatter | solution.py:291
  610.9 400.7 %reduce-scatter.20.cloned.1.call-start = ((), (), s32[]{:S(2)}) async-start(), calls=%async_computation.15 | async-start | bytes 9437184 | tf_op jit(solution)/shard_map/reduce_scatter | solution.py:301
  624.8 462.1 %reduce-scatter.18.cloned.1.call-start = ((), (), s32[]{:S(2)}) async-start(), calls=%async_computation.14 | async-start | bytes 9437184 | tf_op jit(solution)/shard_map/reduce_scatter | solution.py:300
  634.1 105.3 %copy-start.8 = (f32[394,512]{1,0:T(8,128)S(1)}, f32[394,512]{1,0:T(8,128)}, u32[]{:S(2)}) copy-start(f32[394,512]{1,0:T(8,128)} %copy-done.7) | copy-start | bytes 2420740
  (55 other events, 1251.8 us)
Sparse Core Ops, SparseCore 0:
  12.3 57.8 all-gather.8
  561.5 134.5 reduce-scatter.21
  698.9 133.2 reduce-scatter.15
  838.1 99.1 reduce-scatter.13
  941.2 70.3 reduce-scatter.19
  1015.5 71.3 reduce-scatter.17
Sparse Core Ops, SparseCore 1:
  82.1 39.9 all-gather.16
  125.1 38.8 all-gather.14
  165.7 35.4 all-gather.10
  203.0 36.5 all-gather.12
